TPU v7x, 32 devices: a whole 2x2x4 slice. The times are simulated.
32 devices in a mesh: grp: 4 (over y, core), span: 8 (over z, x).
Axes of the slice: x: 2, y: 2, z: 4, core: 2. Of those that a mesh axis runs over, the one named last changes fastest.
Arguments:
- record: float32 [131072, 128], P(('grp', 'span')), may hold values from -96 to 96, as said below
Outputs:
- triangle: float32 [512, 512], replicated
- operator: float32 [512, 512], replicated
Inputs may be any that keep to these rules, and one draw needn't show every extreme that they name: `record`: Real-valued probe samples.
All inputs are finite; a program needn't handle non-finite values.
Results may differ from a plain program's by a relative error of at most 0.0003.
Values sent between devices are 32-bit elements; how exact they have to be, the bound alone decides.
A program may use at most 64 MiB of HBM per device.

v0:
```python
import jax
import jax.numpy as jnp
from jax import lax
from jax.sharding import PartitionSpec as P

LAGS = 4
DELAY = 1024


def shifted(value, axis, steps):
    count = lax.axis_size(axis)
    leading, last = (max(0, -steps), min(count, count - steps))
    return lax.ppermute(value, axis, [(source, source + steps) for source in range(leading, last)])


def inner_rows(left, right):
    return lax.dot_general(
        left,
        right,
        (((0,), (0,)), ((), ())),
        precision=lax.Precision.HIGHEST,
        preferred_element_type=jnp.float32,
    )


def on_device(record):
    count = record.shape[0]
    lead = (LAGS - 1) * DELAY + 1
    following = shifted(record[:lead], ("grp", "span"), -1)
    ext = jnp.concatenate([record, following], 0)
    hank = jnp.concatenate([ext[k * DELAY : k * DELAY + count + 1] for k in range(LAGS)], 1)
    devices = lax.axis_size(("grp", "span"))
    last_row = count * devices - lead
    times = lax.axis_index(("grp", "span")) * count + jnp.arange(count, dtype=jnp.int32)
    weight = (
        jnp.where(times < last_row, 1.0, 0.0)
        - 0.5 * jnp.where(times == 0, 1.0, 0.0)
        - 0.5 * jnp.where(times == last_row, 1.0, 0.0)
    )
    weight = weight.astype(jnp.float32)
    inside = jnp.where(times < last_row, 1.0, 0.0).astype(jnp.float32)
    head = hank[:count]
    weighted = head * weight[:, None]
    cross = inner_rows(head * inside[:, None], hank[1 : count + 1])
    scale = 1.0 / last_row
    gram = inner_rows(weighted, head)
    gram, cross = lax.psum((gram, cross), ("grp", "span"))
    lower = jnp.linalg.cholesky(gram * scale)
    middle = jax.scipy.linalg.solve_triangular(lower, cross * scale, lower=True)
    operator = jax.scipy.linalg.solve_triangular(lower, middle.T, lower=True).T
    return (lower.T, operator)


def solution(mesh):
    placed = (P(("grp", "span"), None),)
    return jax.shard_map(
        on_device, mesh=mesh, in_specs=placed, out_specs=(P(), P()), check_vma=False
    )
```

profile of v0, /device:TPU:0, one launch (start us, length us, event | category | flops | bytes accessed | tf_op | source)
XLA Modules:
  0.0 379.2 jit_solution(13203362706034608490)
XLA Ops:
  7.2 1.5 slice.124
  8.7 1.3 collective-permute-start
  10.0 1.7 constant_dynamic-update-slice_fusion.1
  11.8 36.3 %collective-permute-done = f32[3073,128]{1,0:T(8,128)S(1)} collective-permute-done((f32[3073,128]{1,0:T(8,128)S(1)}, f32[3073,128]{1,0:T(8,128)S(1)}, u32[]{:S(2)}, u32[]{:S(2)}) %collective-permute-start) | collective-permute-done | bytes 1573408 | tf_op jit(solution)/shard_map/ppermute | solution.py:13
  48.7 1.4 pad_maximum_fusion
  50.1 17.3 %fusion.2 = f32[512,512]{0,1:T(8,128)} fusion(f32[4097,512]{1,0:T(8,128)S(1)} %pad_maximum_fusion, f32[4096]{0:T(1024)S(1)} %get-tuple-element.52), kind=kOutput, calls=%fused_computation.5 | convolution fusion | flops 12886999040 | bytes 17842176 | tf_op jit(solution)/shard_map/dot_general | solution.py:17
  67.4 16.4 %fusion = f32[512,512]{0,1:T(8,128)} fusion(f32[4097,512]{1,0:T(8,128)S(1)} %pad_maximum_fusion, f32[4096]{0:T(1024)S(1)} %get-tuple-element.51), kind=kOutput, calls=%fused_computation.2 | convolution fusion | flops 12886999040 | bytes 17842176 | tf_op jit(solution)/shard_map/dot_general | solution.py:17
  83.8 139.5 %all-reduce.4.cloned.1.call-done = (f32[512,512]{0,1:T(8,128)}, f32[512,512]{0,1:T(8,128)}) async-done(((f32[512,512]{0,1:T(8,128)}, f32[512,512]{0,1:T(8,128)}), (f32[512,512]{0,1:T(8,128)}, f32[512,512]{0,1:T(8,128)})) %all-reduce.4.cloned.1.call-update) | async-done | bytes 2097168 | tf_op jit(solution)/shard_map/psum | solution.py:47
  223.3 1.3 broadcast_multiply_fusion.1
  225.0 1.5 fusion.9
  226.5 11.7 %cholesky.104 = f32[128,128]{1,0:T(8,128)S(1)} custom-call(f32[128,128]{1,0:T(8,128)S(1)} %cholesky.266), custom_call_target="Cholesky" | custom-call | tf_op jit(solution)/shard_map/jit(cholesky)/cholesky | solution.py:48
  238.2 9.8 %custom-call.30 = f32[1,128,128]{1,2,0:T(8,128)S(1)} custom-call(f32[1,128,128]{2,1,0:T(8,128)S(1)} %get-tuple-element.48), custom_call_target="InvertDiagBlocksLowerTriangular" | custom-call | tf_op jit(solution)/shard_map/jit(cholesky)/cholesky | solution.py:48
  248.8 12.2 %cholesky.217 = f32[128,128]{1,0:T(8,128)S(1)} custom-call(f32[128,128]{1,0:T(8,128)S(1)} %cholesky.270), custom_call_target="Cholesky" | custom-call | tf_op jit(solution)/shard_map/jit(cholesky)/cholesky | solution.py:48
  262.3 9.8 %custom-call.31 = f32[1,128,128]{1,2,0:T(8,128)S(1)} custom-call(f32[1,128,128]{2,1,0:T(8,128)S(1)} %get-tuple-element.45), custom_call_target="InvertDiagBlocksLowerTriangular" | custom-call | tf_op jit(solution)/shard_map/jit(cholesky)/cholesky | solution.py:48
  272.8 11.7 %cholesky.238 = f32[128,128]{1,0:T(8,128)S(1)} custom-call(f32[128,128]{1,0:T(8,128)S(1)} %cholesky.275), custom_call_target="Cholesky" | custom-call | tf_op jit(solution)/shard_map/jit(cholesky)/cholesky | solution.py:48
  284.5 0.7 compare_reduce_fusion.1
  285.2 9.8 %custom-call.32 = f32[1,128,128]{1,2,0:T(8,128)S(1)} custom-call(f32[1,128,128]{2,1,0:T(8,128)S(1)} %get-tuple-element.42), custom_call_target="InvertDiagBlocksLowerTriangular" | custom-call | tf_op jit(solution)/shard_map/jit(cholesky)/cholesky | solution.py:48
  295.7 11.9 %cholesky.255 = f32[128,128]{1,0:T(8,128)S(1)} custom-call(f32[128,128]{1,0:T(8,128)S(1)} %convolution_subtract_fusion.8), custom_call_target="Cholesky" | custom-call | tf_op jit(solution)/shard_map/jit(cholesky)/cholesky | solution.py:48
  307.6 0.6 compare_reduce_fusion
  311.0 8.0 %while.4 = (s32[]{:T(128)}, f32[512,512]{1,0:T(8,128)S(1)}, s32[4,2]{0,1:T(2,128)S(1)}, f32[4,128,128]{2,1,0:T(8,128)S(1)}, s32[]{:T(128)}) while((s32[]{:T(128)}, f32[512,512]{1,0:T(8,128)S(1)}, s32[4,2]{0,1:T(2,128)S(1)}, f32[4,128,128]{2,1,0:T(8,128)S(1)}, s32[]{:T(128)}) %tuple.41), condition=%wide.while_cond.clone, body=%wide.while_body.clone.sunk | while | flops 2 | bytes 131181 | solution.py:50
  311.6 1.4 bitcast_dynamic-update-slice_fusion.2
  313.6 1.4 bitcast_dynamic-update-slice_fusion.2
  315.6 1.4 bitcast_dynamic-update-slice_fusion.2
  317.6 1.4 bitcast_dynamic-update-slice_fusion.2
  319.0 39.3 %custom-call.35 = f32[4,128,128]{1,2,0:T(8,128)S(1)} custom-call(f32[4,128,128]{2,1,0:T(8,128)S(1)} %get-tuple-element.18), custom_call_target="InvertDiagBlocksLowerTriangular" | custom-call | tf_op jit(solution)/shard_map/jit(_solve_triangular)/triangular_solve | solution.py:50
  358.4 1.3 broadcast_multiply_fusion
  361.2 1.0 convolution_subtract_fusion.2
  362.6 1.5 convolution_subtract_fusion.5
  366.1 1.0 convolution_subtract_fusion
  367.5 1.5 convolution_subtract_fusion.4
  369.5 1.3 copy.7
  370.8 1.3 copy.6
  (46 shorter events, 11.8 us)
Async XLA Ops:
  7.2 216.1 %all-reduce.4.cloned.1.call-start = ((), (), s32[]{:S(2)}) async-start(), calls=%async_computation | async-start | bytes 4194304 | tf_op jit(solution)/shard_map/psum | solution.py:47
  8.7 39.3 %collective-permute-start = (f32[3073,128]{1,0:T(8,128)S(1)}, f32[3073,128]{1,0:T(8,128)S(1)}, u32[]{:S(2)}, u32[]{:S(2)}) collective-permute-start(f32[3073,128]{1,0:T(8,128)S(1)} %slice.124), channel_id=1, source_target_pairs={{1,0},{2,1},{3,2},{4,3},{5,4},{6,5},{7,6},{8,7},{9,8},{10,9},{11,1... | collective-permute-start | bytes 4720136 | tf_op jit(solution)/shard_map/ppermute | solution.py:13
Sparse Core Ops, SparseCore 0:
  83.9 139.3 all-reduce.3
where the time goes:
time: 384 us; the launch traced here: 379 us
  waiting for transfers between devices  176 us (46%)
  other arithmetic  125 us (33%)
  matrix products  45 us (12%)
  between operations  17.1 us (4%)
  local copies, waits for them, and re-layouts  14.9 us (4%)
    psum x1, waiting for transfers between devices, on_device(): gram, cross = lax.psum((gram, cross), ('grp', 'span'))  140 us
    another operation x15, other arithmetic, on_device(): lower = jnp.linalg.cholesky(gram * scale)  79.7 us
    another operation x4, other arithmetic, on_device(): operator = jax.scipy.linalg.solve_triangular(lower, middle.T, lower=True).T  39.6 us
    ppermute x1, waiting for transfers between devices, shifted(): lax.ppermute(value, axis, [(source, source + steps) for source in range(l...  36.3 us
    dot_general x2, matrix products, inner_rows(): lax.dot_general(left, right, (((0,), (0,)), ((), ())), precision=lax.Prec...  33.6 us
    another operation x13, local copies, waits for them, and re-layouts, on_device(): operator = jax.scipy.linalg.solve_triangular(lower, middle.T, lower=True).T  7.92 us
  transfers between devices with their start and end apart: 2, of which 2 were waited for; matrix products, arithmetic and copies ran while one was open for 0% of the time, Pallas kernels for 0%

commit v1 on v0

--- a/solution.py
+++ b/solution.py
@@ -44,7 +44,7 @@
     cross = inner_rows(head * inside[:, None], hank[1 : count + 1])
     scale = 1.0 / last_row
     gram = inner_rows(weighted, head)
-    gram, cross = lax.psum((gram, cross), ("grp", "span"))
+    gram, cross = lax.psum(lax.psum((gram, cross), axis_name="grp"), axis_name="span")
     lower = jnp.linalg.cholesky(gram * scale)
     middle = jax.scipy.linalg.solve_triangular(lower, cross * scale, lower=True)
     operator = jax.scipy.linalg.solve_triangular(lower, middle.T, lower=True).T

time: 384 us -> 407 us (1.060)
  waiting for transfers between devices: 176 us -> 199 us
    psum x1 -> x2, waiting for transfers between devices: 140 us -> 162 us  [the longest x1 106 us: on_device(): lax.psum(lax.psum((gram, cross), axis_name='grp'), axis_name='span')]
  transfers between devices with their start and end apart: 2 -> 3, of which waited for: 2 -> 3; matrix products, arithmetic and copies ran while one was open for 0% -> 0% of each run, Pallas kernels for 0% -> 0%
where the time goes in v1:
time: 407 us; the launch traced here: 402 us
  waiting for transfers between devices  199 us (49%)
  other arithmetic  125 us (31%)
  matrix products  45.2 us (11%)
  between operations  17.2 us (4%)
  local copies, waits for them, and re-layouts  14.9 us (4%)
    psum x1, waiting for transfers between devices, on_device(): lax.psum(lax.psum((gram, cross), axis_name='grp'), axis_name='span')  106 us
    another operation x15, other arithmetic, on_device(): lower = jnp.linalg.cholesky(gram * scale)  79.4 us
    psum x1, waiting for transfers between devices, on_device(): lax.psum((gram, cross), axis_name='grp')  56.2 us
    another operation x4, other arithmetic, on_device(): operator = jax.scipy.linalg.solve_triangular(lower, middle.T, lower=True).T  39.6 us
    ppermute x1, waiting for transfers between devices, shifted(): lax.ppermute(value, axis, [(source, source + steps) for source in range(l...  36.3 us
    dot_general x2, matrix products, inner_rows(): lax.dot_general(left, right, (((0,), (0,)), ((), ())), precision=lax.Prec...  33.8 us
  transfers between devices with their start and end apart: 3, of which 3 were waited for; matrix products, arithmetic and copies ran while one was open for 0% of the time, Pallas kernels for 0%

profile of v1, /device:TPU:0, one launch (start us, length us, event | category | flops | bytes accessed | tf_op | source)
XLA Modules:
  0.0 401.9 jit_solution(15200298157195339105)
XLA Ops:
  7.2 1.5 slice.124
  8.7 1.3 collective-permute-start
  10.0 1.7 constant_dynamic-update-slice_fusion.1
  11.8 36.3 %collective-permute-done = f32[3073,128]{1,0:T(8,128)S(1)} collective-permute-done((f32[3073,128]{1,0:T(8,128)S(1)}, f32[3073,128]{1,0:T(8,128)S(1)}, u32[]{:S(2)}, u32[]{:S(2)}) %collective-permute-start) | collective-permute-done | bytes 1573408 | tf_op jit(solution)/shard_map/ppermute | solution.py:13
  48.7 1.4 pad_maximum_fusion
  50.1 17.3 %fusion.2 = f32[512,512]{0,1:T(8,128)} fusion(f32[4097,512]{1,0:T(8,128)S(1)} %pad_maximum_fusion, f32[4096]{0:T(1024)S(1)} %get-tuple-element.54), kind=kOutput, calls=%fused_computation.5 | convolution fusion | flops 12886999040 | bytes 17842176 | tf_op jit(solution)/shard_map/dot_general | solution.py:17
  67.4 16.5 %fusion = f32[512,512]{0,1:T(8,128)} fusion(f32[4097,512]{1,0:T(8,128)S(1)} %pad_maximum_fusion, f32[4096]{0:T(1024)S(1)} %get-tuple-element.53), kind=kOutput, calls=%fused_computation.2 | convolution fusion | flops 12886999040 | bytes 17842176 | tf_op jit(solution)/shard_map/dot_general | solution.py:17
  84.0 56.2 %all-reduce.8.cloned.1.call-done = (f32[512,512]{0,1:T(8,128)}, f32[512,512]{0,1:T(8,128)}) async-done(((f32[512,512]{0,1:T(8,128)}, f32[512,512]{0,1:T(8,128)}), (f32[512,512]{0,1:T(8,128)}, f32[512,512]{0,1:T(8,128)})) %all-reduce.8.cloned.1.call-update) | async-done | bytes 2097168 | tf_op jit(solution)/shard_map/psum | solution.py:47
  140.3 106.0 %all-reduce.6.cloned.1.call-done = (f32[512,512]{0,1:T(8,128)}, f32[512,512]{0,1:T(8,128)}) async-done(((f32[512,512]{0,1:T(8,128)}, f32[512,512]{0,1:T(8,128)}), (f32[512,512]{0,1:T(8,128)}, f32[512,512]{0,1:T(8,128)})) %all-reduce.6.cloned.1.call-update) | async-done | bytes 2097168 | tf_op jit(solution)/shard_map/psum | solution.py:47
  246.3 1.3 broadcast_multiply_fusion.1
  248.0 1.5 fusion.9
  249.4 11.7 %cholesky.104 = f32[128,128]{1,0:T(8,128)S(1)} custom-call(f32[128,128]{1,0:T(8,128)S(1)} %cholesky.266), custom_call_target="Cholesky" | custom-call | tf_op jit(solution)/shard_map/jit(cholesky)/cholesky | solution.py:48
  261.3 9.8 %custom-call.30 = f32[1,128,128]{1,2,0:T(8,128)S(1)} custom-call(f32[1,128,128]{2,1,0:T(8,128)S(1)} %get-tuple-element.50), custom_call_target="InvertDiagBlocksLowerTriangular" | custom-call | tf_op jit(solution)/shard_map/jit(cholesky)/cholesky | solution.py:48
  271.8 11.7 %cholesky.217 = f32[128,128]{1,0:T(8,128)S(1)} custom-call(f32[128,128]{1,0:T(8,128)S(1)} %cholesky.270), custom_call_target="Cholesky" | custom-call | tf_op jit(solution)/shard_map/jit(cholesky)/cholesky | solution.py:48
  284.8 9.9 %custom-call.31 = f32[1,128,128]{1,2,0:T(8,128)S(1)} custom-call(f32[1,128,128]{2,1,0:T(8,128)S(1)} %get-tuple-element.47), custom_call_target="InvertDiagBlocksLowerTriangular" | custom-call | tf_op jit(solution)/shard_map/jit(cholesky)/cholesky | solution.py:48
  295.5 11.7 %cholesky.238 = f32[128,128]{1,0:T(8,128)S(1)} custom-call(f32[128,128]{1,0:T(8,128)S(1)} %cholesky.275), custom_call_target="Cholesky" | custom-call | tf_op jit(solution)/shard_map/jit(cholesky)/cholesky | solution.py:48
  307.2 0.7 compare_reduce_fusion.1
  307.9 9.8 %custom-call.32 = f32[1,128,128]{1,2,0:T(8,128)S(1)} custom-call(f32[1,128,128]{2,1,0:T(8,128)S(1)} %get-tuple-element.44), custom_call_target="InvertDiagBlocksLowerTriangular" | custom-call | tf_op jit(solution)/shard_map/jit(cholesky)/cholesky | solution.py:48
  318.3 11.9 %cholesky.255 = f32[128,128]{1,0:T(8,128)S(1)} custom-call(f32[128,128]{1,0:T(8,128)S(1)} %convolution_subtract_fusion.8), custom_call_target="Cholesky" | custom-call | tf_op jit(solution)/shard_map/jit(cholesky)/cholesky | solution.py:48
  333.7 8.0 %while.4 = (s32[]{:T(128)}, f32[512,512]{1,0:T(8,128)S(1)}, s32[4,2]{0,1:T(2,128)S(1)}, f32[4,128,128]{2,1,0:T(8,128)S(1)}, s32[]{:T(128)}) while((s32[]{:T(128)}, f32[512,512]{1,0:T(8,128)S(1)}, s32[4,2]{0,1:T(2,128)S(1)}, f32[4,128,128]{2,1,0:T(8,128)S(1)}, s32[]{:T(128)}) %tuple.41), condition=%wide.while_cond.clone, body=%wide.while_body.clone.sunk | while | flops 2 | bytes 131181 | solution.py:50
  334.4 1.4 bitcast_dynamic-update-slice_fusion.2
  336.4 1.4 bitcast_dynamic-update-slice_fusion.2
  338.4 1.4 bitcast_dynamic-update-slice_fusion.2
  340.4 1.4 bitcast_dynamic-update-slice_fusion.2
  341.8 39.3 %custom-call.35 = f32[4,128,128]{1,2,0:T(8,128)S(1)} custom-call(f32[4,128,128]{2,1,0:T(8,128)S(1)} %get-tuple-element.18), custom_call_target="InvertDiagBlocksLowerTriangular" | custom-call | tf_op jit(solution)/shard_map/jit(_solve_triangular)/triangular_solve | solution.py:50
  381.1 1.3 broadcast_multiply_fusion
  383.9 1.0 convolution_subtract_fusion.2
  385.3 1.5 convolution_subtract_fusion.5
  388.8 1.0 convolution_subtract_fusion
  390.2 1.5 convolution_subtract_fusion.4
  392.2 1.3 copy.7
  393.5 1.3 copy.6
  (49 shorter events, 12.5 us)
Async XLA Ops:
  7.2 133.1 %all-reduce.8.cloned.1.call-start = ((), (), s32[]{:S(2)}) async-start(), calls=%async_computation.1 | async-start | bytes 4194304 | tf_op jit(solution)/shard_map/psum | solution.py:47
  8.7 39.3 %collective-permute-start = (f32[3073,128]{1,0:T(8,128)S(1)}, f32[3073,128]{1,0:T(8,128)S(1)}, u32[]{:S(2)}, u32[]{:S(2)}) collective-permute-start(f32[3073,128]{1,0:T(8,128)S(1)} %slice.124), channel_id=1, source_target_pairs={{1,0},{2,1},{3,2},{4,3},{5,4},{6,5},{7,6},{8,7},{9,8},{10,9},{11,1... | collective-permute-start | bytes 4720136 | tf_op jit(solution)/shard_map/ppermute | solution.py:13
  83.9 162.3 %all-reduce.6.cloned.1.call-start = ((), (), s32[]{:S(2)}) async-start(), calls=%async_computation | async-start | bytes 4194304 | tf_op jit(solution)/shard_map/psum | solution.py:47
Sparse Core Ops, SparseCore 0:
  84.1 56.1 all-reduce.7
  143.9 102.3 all-reduce.5
